TPU v7x, 32 devices: a whole 2x2x4 slice. The times are simulated.
32 devices in a mesh: member: 4 (over x, core), space: 8 (over z, y).
Axes of the slice: x: 2, y: 2, z: 4, core: 2. Of those that a mesh axis runs over, the one named last changes fastest.
Arguments:
- features: bfloat16 [4, 641, 192, 128], P('member', None, 'space'), may hold values from -6 to 6
- depth_kernel: float32 [641, 5, 5], replicated, may hold values from -1.25 to 1.25
- in_weight: bfloat16 [641, 1282], replicated, may hold values from -0.25 to 0.25
- out_weight: bfloat16 [1282, 641], replicated, may hold values from -0.15625 to 0.15625
- decoder_weight: bfloat16 [641, 72], replicated, may hold values from -0.25 to 0.25
- observed: float32 [72, 192, 128], P(None, 'space'), may hold values from -6 to 6
- land_mask: int32 [192, 128], P('space'), may hold values 0 or 1
Outputs:
- grad_features: bfloat16 [4, 641, 192, 128], P('member', None, 'space')
- decoder_grad: float32 [641, 72], replicated
All inputs are finite; a program needn't handle non-finite values. No bound on the sum of `land_mask` on one device may be relied on, other than what follows from the above.
Results may differ from a plain program's by a relative error of at most 0.0054.
Values may be sent and summed in bfloat16 or wider, within the bound.
A program may use at most 128 MiB of HBM per device.

v0:
```python
import math
import jax
import jax.numpy as jnp
from jax import lax
from jax.sharding import PartitionSpec as P

norm_eps = 1e-05


def padded_2(cells, sides, width):
    for axis, dim in sides:
        count = lax.axis_size(axis)
        head = lax.slice_in_dim(cells, 0, width, axis=dim)
        tail = lax.slice_in_dim(cells, cells.shape[dim] - width, cells.shape[dim], axis=dim)
        cells = jnp.concatenate(
            [
                lax.ppermute(tail, axis, [(i, (i + 1) % count) for i in range(count)]),
                cells,
                lax.ppermute(head, axis, [((i + 1) % count, i) for i in range(count)]),
            ],
            axis=dim,
        )
    return cells


def per_device(features, depth_kernel, in_weight, out_weight, decoder_weight, observed, land_mask):
    channels = features.shape[1]
    lon_len = features.shape[2]
    lat_len = features.shape[3]
    points = lon_len * lat_len
    padded = padded_2(features, (("space", 2),), 2)
    widened = jnp.pad(padded.astype(jnp.float32), ((0, 0), (0, 0), (0, 0), (2, 2)))
    convolved = jnp.zeros(features.shape, jnp.float32)
    for row_off in range(5):
        for col_off in range(5):
            convolved = (
                convolved
                + depth_kernel[:, row_off, col_off][None, :, None, None]
                * widened[:, :, row_off : row_off + lon_len, col_off : col_off + lat_len]
            )
    center = jnp.mean(convolved, axis=1, keepdims=True)
    shifted = convolved - center
    normed = (
        shifted * lax.rsqrt(jnp.mean(shifted * shifted, axis=1, keepdims=True) + norm_eps)
    ).astype(jnp.bfloat16)
    flat = normed.reshape(channels, points)
    hidden = jax.nn.gelu(
        jnp.einsum("ch,cp->hp", in_weight, flat, preferred_element_type=jnp.float32),
        approximate=False,
    ).astype(jnp.bfloat16)
    mlp_out = jnp.einsum("hc,hp->cp", out_weight, hidden, preferred_element_type=jnp.float32)
    block_out = (features.reshape(channels, points).astype(jnp.float32) + mlp_out).astype(
        jnp.bfloat16
    )
    decoded_flat = jnp.einsum(
        "co,cp->op", decoder_weight, block_out, preferred_element_type=jnp.float32
    ).astype(jnp.bfloat16)
    outputs = decoded_flat.shape[0]
    decoded = decoded_flat.reshape(1, outputs, lon_len, lat_len)
    groups = lax.axis_size("member")
    members = features.shape[0] * groups
    point_weight = 4.0 + 8.0 * land_mask.astype(jnp.float32)
    own_f = decoded.astype(jnp.float32)
    apart = own_f - lax.all_gather(decoded, "member", axis=0, tiled=True).astype(jnp.float32)
    apart_norm = jnp.sqrt(jnp.sum(apart * apart, axis=1, keepdims=True) + 1.0)
    pair_sum = jnp.sum(apart / apart_norm, axis=0, keepdims=True)
    misfit = own_f - observed[None]
    misfit_norm = jnp.sqrt(jnp.sum(misfit * misfit, axis=1, keepdims=True) + 1.0)
    score_grad = (point_weight[None, None] * (misfit / misfit_norm - pair_sum / members)).astype(
        jnp.bfloat16
    )
    grad_flat = score_grad.reshape(outputs, points)
    grad_features = jnp.einsum(
        "co,op->cp", decoder_weight, grad_flat, preferred_element_type=jnp.float32
    ).astype(jnp.bfloat16)
    total_points = lon_len * lax.axis_size("space") * lat_len
    term = jnp.einsum(
        "cp,op->co", block_out, grad_flat, preferred_element_type=jnp.float32
    ) / math.sqrt(members * total_points)
    decoder_grad = lax.psum(term, ("member", "space"))
    return (grad_features.reshape(features.shape), decoder_grad)


def solution(mesh):
    placed = (
        P("member", None, "space", None),
        P(),
        P(),
        P(),
        P(),
        P(None, "space", None),
        P("space", None),
    )
    return jax.shard_map(
        per_device,
        mesh=mesh,
        in_specs=placed,
        out_specs=(P("member", None, "space", None), P()),
        check_vma=False,
    )
```

profile of v0, /device:TPU:8, one launch (start us, length us, event | category | flops | bytes accessed | tf_op | source)
XLA Modules:
  0.0 393.1 jit_solution(12034791294327075821)
XLA Ops:
  7.2 0.0 copy-start
  7.2 0.0 all-gather.2.cloned.1.call-start
  7.2 2.3 fusion.106
  9.6 1.6 collective-permute-start
  11.3 1.5 collective-permute-start.1
  12.7 2.6 convert_bitcast_fusion
  15.3 0.5 pad.8
  15.9 0.0 copy-start.8
  15.9 0.0 copy-start.5
  15.9 5.0 %copy.15 = f32[81,8,24,128]{3,1,2,0:T(8,128)} copy(f32[81,8,24,128]{3,2,1,0:T(8,128)S(1)} %bitcast.131) | data formatting | bytes 15925248
  20.9 0.1 slice_reduce_fusion.23
  21.0 0.2 slice_reduce_fusion.24
  21.1 4.2 %collective-permute-done = bf16[1,641,2,128]{3,1,2,0:T(8,128)(2,1)S(1)} collective-permute-done((bf16[1,641,2,128]{3,1,2,0:T(8,128)(2,1)S(1)}, bf16[1,641,2,128]{3,1,2,0:T(8,128)(2,1)S(1)}, u32[]{:S(2)}, u32[]{:S(2)}) %collective-permute-start) | collective-permute-done | bytes 328224 | tf_op jit(solution)/shard_map/ppermute | solution.py:17
  25.4 0.3 copy.11
  25.6 1.6 collective-permute-done.1
  27.2 0.3 copy.12
  27.5 6.9 %maximum_convert_fusion = f32[1,641,28,128]{3,2,1,0:T(8,128)} fusion(bf16[1,641,2,128]{3,2,1,0:T(2,128)(2,1)S(1)} %copy.12, bf16[1,641,24,128]{3,2,1,0:T(8,128)(2,1)S(1)} %copy-done.5, bf16[1,641,2,128]{3,2,1,0:T(2,128)(2,1)S(1)} %copy.11), kind=kLoop, calls=%fused_computation.100 | loop fusion | flops 13784064 | bytes 13784064 | tf_op jit(solution)/shard_map/convert_element_type | solution.py:32
  34.4 130.6 %fusion.104 = (f32[24,128]{1,0:T(8,128)S(1)}, f32[1,641,24,128]{3,2,1,0:T(8,128)}) fusion(f32[641]{0:T(1024)S(1)} %get-tuple-element.25, f32[641]{0:T(1024)S(1)} %get-tuple-element.26, f32[1,641,28,128]{3,2,1,0:T(8,128)} %maximum_convert_fusion, f32[641]{0:T(1024)S(1)} %get-tuple-element.3, f32[641]{0:T(1024)S(1)} %get-tuple-element.4, ...), kind=kLoop, calls=%fused_computation.177 | loop fusion | flops 98454528 | bytes 57838180 | tf_op jit(solution)/shard_map/reduce_sum | solution.py:41
  165.0 4.3 %multiply_reduce_fusion = f32[24,128]{1,0:T(8,128)S(1)} fusion(f32[1,641,24,128]{3,2,1,0:T(8,128)} %get-tuple-element.28, f32[24,128]{1,0:T(8,128)S(1)} %broadcast_multiply_fusion), kind=kLoop, calls=%fused_computation.99 | loop fusion | flops 5904384 | bytes 7901184 | tf_op jit(solution)/shard_map/reduce_sum | solution.py:44
  169.3 1.1 copy-done.2
  170.4 0.9 fusion.69
  171.3 0.7 pad.9
  172.0 0.0 slice-start
  172.0 1.1 copy.16
  173.2 0.0 copy-start.10
  173.2 42.9 %fusion.123 = bf16[1282,3072]{1,0:T(8,128)(2,1)S(1)} fusion(bf16[641,3072]{1,0:T(8,128)(2,1)S(1)} %bitcast.142, bf16[641,1282]{1,0:T(8,128)(2,1)S(1)} %copy-done), kind=kOutput, calls=%fused_computation.23.clone.clone.clone.clone.1 | convolution fusion | flops 5304895488 | bytes 13458436 | tf_op jit(solution)/shard_map/ch,cp->hp/dot_general | solution.py:48
  216.1 0.0 copy-start.7
  216.2 7.2 %fusion.18 = bf16[641,3072]{1,0:T(8,128)(2,1)S(1)} fusion(f32[641,3072]{1,0:T(8,128)S(1)} %bitcast.138, bf16[1282,641]{0,1:T(8,128)(2,1)S(1)} %copy-done.10, bf16[1282,3072]{1,0:T(8,128)(2,1)S(1)} %fusion.123), kind=kOutput, calls=%fused_computation.45 | convolution fusion | flops 5052844032 | bytes 21335044 | tf_op jit(solution)/shard_map/hc,hp->cp/dot_general | solution.py:51
  223.4 1.9 copy-done.3
  225.3 0.8 convolution_convert_fusion.1
  226.1 0.8 copy.18
  226.9 0.0 all-gather.2.cloned.1.call-update
  226.9 0.0 all-reduce.3.cloned.1.call-start
  227.0 0.1 convert_bitcast_fusion.1
  227.1 0.2 copy.17
  227.2 0.2 multiply_reduce_fusion.2
  227.4 20.9 %all-gather.2.cloned.1.call-done = bf16[4,72,24,128]{3,2,1,0:T(8,128)(2,1)} async-done(((bf16[1,72,24,128]{3,2,1,0:T(8,128)(2,1)}), bf16[4,72,24,128]{3,2,1,0:T(8,128)(2,1)}) %all-gather.2.cloned.1.call-update) | async-done | bytes 1769488 | tf_op jit(solution)/shard_map/all_gather | solution.py:64
  248.4 2.1 multiply_reduce_fusion.1
  250.5 2.0 divide_reduce_fusion
  252.5 0.2 multiply_convert_fusion.1
  252.7 2.0 convolution_multiply_fusion
  254.7 3.1 convolution_convert_fusion
  257.9 0.0 all-reduce.3.cloned.1.call-update
  257.9 0.0 copy-start.1
  257.9 3.4 copy.20
  261.3 2.6 slice_bitcast_fusion
  263.9 120.7 %all-reduce.3.cloned.1.call-done = f32[641,72]{0,1:T(8,128)} async-done(((f32[641,72]{0,1:T(8,128)}), f32[641,72]{0,1:T(8,128)}) %all-reduce.3.cloned.1.call-update) | async-done | bytes 184624 | tf_op jit(solution)/shard_map/psum | solution.py:80
  384.6 1.6 copy.30
  (24 shorter events, 0.2 us)
Async XLA Ops:
  7.2 166.0 %copy-start = (bf16[641,1282]{1,0:T(8,128)(2,1)S(1)}, bf16[641,1282]{1,0:T(8,128)(2,1)}, u32[]{:S(2)}) copy-start(bf16[641,1282]{1,0:T(8,128)(2,1)} %param.9) | copy-start | bytes 4930576
  7.2 241.2 %all-gather.2.cloned.1.call-start = ((), (), s32[]{:S(2)}) async-start(), calls=%async_computation | async-start | bytes 2211840 | tf_op jit(solution)/shard_map/all_gather | solution.py:64
  9.6 15.7 %collective-permute-start = (bf16[1,641,2,128]{3,1,2,0:T(8,128)(2,1)S(1)}, bf16[1,641,2,128]{3,1,2,0:T(8,128)(2,1)S(1)}, u32[]{:S(2)}, u32[]{:S(2)}) collective-permute-start(bf16[1,641,2,128]{3,1,2,0:T(8,128)(2,1)S(1)} %copy.13), channel_id=1, source_target_pairs={{0,1},{1,2},{2,3},{3,4},{4,5},{5,6},{6,7},{7,0},{8,9},{9,10},{10,1... | collective-permute-start | bytes 984584 | tf_op jit(solution)/shard_map/ppermute | solution.py:17
  11.3 16.0 %collective-permute-start.1 = (bf16[1,641,2,128]{3,1,2,0:T(8,128)(2,1)S(1)}, bf16[1,641,2,128]{3,1,2,0:T(8,128)(2,1)S(1)}, u32[]{:S(2)}, u32[]{:S(2)}) collective-permute-start(bf16[1,641,2,128]{3,1,2,0:T(8,128)(2,1)S(1)} %copy.14), channel_id=1, source_target_pairs={{1,0},{2,1},{3,2},{4,3},{5,4},{6,5},{7,6},{0,7},{9,8},{10,9},{11,1... | collective-permute-start | bytes 984584 | tf_op jit(solution)/shard_map/ppermute | solution.py:19
  15.9 5.0 %copy-start.8 = (f32[641,5,5]{0,2,1:T(8,128)S(1)}, f32[641,5,5]{0,2,1:T(8,128)}, u32[]{:S(2)}) copy-start(f32[641,5,5]{0,2,1:T(8,128)} %param.8) | copy-start | bytes 192304
  15.9 11.6 %copy-start.5 = (bf16[1,641,24,128]{3,2,1,0:T(8,128)(2,1)S(1)}, bf16[1,641,24,128]{3,2,1,0:T(8,128)(2,1)}, u32[]{:S(2)}) copy-start(bf16[1,641,24,128]{3,2,1,0:T(8,128)(2,1)} %param.7) | copy-start | bytes 11814916
  164.9 5.5 %copy-start.2 = (f32[1,641,24,128]{3,2,1,0:T(8,128)S(1)}, f32[1,641,24,128]{3,2,1,0:T(8,128)}, u32[]{:S(2)}) copy-start(f32[1,641,24,128]{3,2,1,0:T(8,128)} %get-tuple-element.28) | copy-start | bytes 23629828
  172.0 44.1 %slice-start = ((s8[7962624]{0:T(1024)(128)(4,1)}), s8[4194304]{0:T(1024)(128)(4,1)S(1)}, s32[]{:S(2)}) async-start(s8[7962624]{0:T(1024)(128)(4,1)} %bitcast.136), calls=%async_computation.2 | async-start | bytes 8388608
  173.1 43.0 %slice-start.1 = ((s8[7962624]{0:T(1024)(128)(4,1)}), s8[3768320]{0:T(1024)(128)(4,1)S(1)}, s32[]{:S(2)}) async-start(s8[7962624]{0:T(1024)(128)(4,1)} %bitcast.136), calls=%async_computation.3 | async-start | bytes 7536640
  173.2 43.0 %copy-start.10 = (bf16[1282,641]{0,1:T(8,128)(2,1)S(1)}, bf16[1282,641]{0,1:T(8,128)(2,1)}, u32[]{:S(2)}) copy-start(bf16[1282,641]{0,1:T(8,128)(2,1)} %param.10) | copy-start | bytes 4930576
  216.1 9.1 %copy-start.7 = (bf16[641,72]{0,1:T(8,128)(2,1)S(1)}, bf16[641,72]{0,1:T(8,128)(2,1)}, u32[]{:S(2)}) copy-start(bf16[641,72]{0,1:T(8,128)(2,1)} %param.11) | copy-start | bytes 276916
  223.4 1.9 copy-start.3
  225.3 1.9 copy-start.6
  225.3 2.1 copy-start.9
  226.9 157.7 %all-reduce.3.cloned.1.call-start = ((), (), s32[]{:S(2)}) async-start(), calls=%async_computation.1 | async-start | bytes 442368 | tf_op jit(solution)/shard_map/psum | solution.py:80
  248.3 4.4 %copy-start.4 = (bf16[641,3072]{1,0:T(8,128)(2,1)S(1)}, bf16[641,3072]{1,0:T(8,128)(2,1)}, u32[]{:S(2)}) copy-start(bf16[641,3072]{1,0:T(8,128)(2,1)} %copy-done.3) | copy-start | bytes 11814916
  257.9 128.3 %copy-start.1 = (bf16[641,1282]{1,0:T(8,128)(2,1)S(1)}, bf16[641,1282]{1,0:T(8,128)(2,1)}, u32[]{:S(2)}) copy-start(bf16[641,1282]{1,0:T(8,128)(2,1)} %param.9) | copy-start | bytes 4930576
Sparse Core Ops, SparseCore 0:
  227.0 21.2 all-gather.1
  258.0 126.5 all-reduce.2
where the time goes:
time: 393 us
  other arithmetic  150 us (38%)
  waiting for transfers between devices  148 us (38%)
  matrix products  56.1 us (14%)
  local copies, waits for them, and re-layouts  22.2 us (6%)
  between operations  14.3 us (4%)
    reduce_sum x1, other arithmetic, per_device(): center = jnp.mean(convolved, axis=1, keepdims=True)  131 us
    psum x1, waiting for transfers between devices, per_device(): decoder_grad = lax.psum(term, ('member', 'space'))  121 us
    dot_general x1, matrix products, per_device(): jnp.einsum('ch,cp->hp', in_weight, flat, preferred_element_type=jnp.float32)  42.9 us
    all_gather x1, waiting for transfers between devices, per_device(): lax.all_gather(decoded, 'member', axis=0, tiled=True).astype(jnp.float32)  20.9 us
    unnamed x36, local copies, waits for them, and re-layouts  16.6 us
  transfers between devices with their start and end apart: 4, of which 4 were waited for; matrix products, arithmetic and copies ran while one was open for 4% of the time, Pallas kernels for 0%

commit v1 on v0

--- a/solution.py
+++ b/solution.py
@@ -77,7 +77,7 @@
     term = jnp.einsum(
         "cp,op->co", block_out, grad_flat, preferred_element_type=jnp.float32
     ) / math.sqrt(members * total_points)
-    decoder_grad = lax.psum(term, ("member", "space"))
+    decoder_grad = lax.psum(lax.psum(term, "space"), "member")
     return (grad_features.reshape(features.shape), decoder_grad)
 
 

time: 393 us -> 369 us (0.939)
  waiting for transfers between devices: 148 us -> 122 us
    psum x1 -> x2, waiting for transfers between devices: 121 us -> 95.5 us  [per_device(): decoder_grad = lax.psum(lax.psum(term, 'space'), 'member')]
  transfers between devices with their start and end apart: 4 -> 5, of which waited for: 4 -> 5; matrix products, arithmetic and copies ran while one was open for 4% -> 5% of each run, Pallas kernels for 0% -> 0%
where the time goes in v1:
time: 369 us; the launch traced here: 368 us
  other arithmetic  150 us (41%)
  waiting for transfers between devices  122 us (33%)
  matrix products  54.2 us (15%)
  local copies, waits for them, and re-layouts  24 us (7%)
  between operations  14 us (4%)
    reduce_sum x1, other arithmetic, per_device(): center = jnp.mean(convolved, axis=1, keepdims=True)  131 us
    psum x2, waiting for transfers between devices, per_device(): decoder_grad = lax.psum(lax.psum(term, 'space'), 'member')  95.5 us
    dot_general x1, matrix products, per_device(): jnp.einsum('ch,cp->hp', in_weight, flat, preferred_element_type=jnp.float32)  42.9 us
    all_gather x1, waiting for transfers between devices, per_device(): lax.all_gather(decoded, 'member', axis=0, tiled=True).astype(jnp.float32)  20.9 us
    unnamed x36, local copies, waits for them, and re-layouts  16.2 us
  transfers between devices with their start and end apart: 5, of which 5 were waited for; matrix products, arithmetic and copies ran while one was open for 5% of the time, Pallas kernels for 0%

profile of v1, /device:TPU:8, one launch (start us, length us, event | category | flops | bytes accessed | tf_op | source)
XLA Modules:
  0.0 367.5 jit_solution(1414615255015293656)
XLA Ops:
  7.2 0.0 copy-start
  7.2 0.0 all-gather.2.cloned.1.call-start
  7.2 2.3 fusion.106
  9.6 1.6 collective-permute-start
  11.3 1.5 collective-permute-start.1
  12.7 2.6 convert_bitcast_fusion
  15.3 0.5 pad.8
  15.9 0.0 copy-start.5
  15.9 5.0 %copy.15 = f32[81,8,24,128]{3,1,2,0:T(8,128)} copy(f32[81,8,24,128]{3,2,1,0:T(8,128)S(1)} %bitcast.131) | data formatting | bytes 15925248
  20.9 0.1 slice_reduce_fusion.23
  21.0 0.2 slice_reduce_fusion.24
  21.1 4.2 %collective-permute-done = bf16[1,641,2,128]{3,1,2,0:T(8,128)(2,1)S(1)} collective-permute-done((bf16[1,641,2,128]{3,1,2,0:T(8,128)(2,1)S(1)}, bf16[1,641,2,128]{3,1,2,0:T(8,128)(2,1)S(1)}, u32[]{:S(2)}, u32[]{:S(2)}) %collective-permute-start) | collective-permute-done | bytes 328224 | tf_op jit(solution)/shard_map/ppermute | solution.py:17
  25.4 0.3 copy.11
  25.6 1.6 collective-permute-done.1
  27.2 0.3 copy.12
  27.5 6.9 %maximum_convert_fusion = f32[1,641,28,128]{3,2,1,0:T(8,128)} fusion(bf16[1,641,2,128]{3,2,1,0:T(2,128)(2,1)S(1)} %copy.12, bf16[1,641,24,128]{3,2,1,0:T(8,128)(2,1)S(1)} %copy-done.5, bf16[1,641,2,128]{3,2,1,0:T(2,128)(2,1)S(1)} %copy.11), kind=kLoop, calls=%fused_computation.100 | loop fusion | flops 13784064 | bytes 13784064 | tf_op jit(solution)/shard_map/convert_element_type | solution.py:32
  34.4 130.5 %fusion.104 = (f32[24,128]{1,0:T(8,128)S(1)}, f32[1,641,24,128]{3,2,1,0:T(8,128)}) fusion(f32[641]{0:T(1024)S(1)} %get-tuple-element.25, f32[641]{0:T(1024)S(1)} %get-tuple-element.26, f32[1,641,28,128]{3,2,1,0:T(8,128)} %maximum_convert_fusion, f32[641]{0:T(1024)S(1)} %get-tuple-element.3, f32[641]{0:T(1024)S(1)} %get-tuple-element.4, ...), kind=kLoop, calls=%fused_computation.177 | loop fusion | flops 98454528 | bytes 57838180 | tf_op jit(solution)/shard_map/reduce_sum | solution.py:41
  164.9 4.3 %multiply_reduce_fusion = f32[24,128]{1,0:T(8,128)S(1)} fusion(f32[1,641,24,128]{3,2,1,0:T(8,128)} %get-tuple-element.28, f32[24,128]{1,0:T(8,128)S(1)} %broadcast_multiply_fusion), kind=kLoop, calls=%fused_computation.99 | loop fusion | flops 5904384 | bytes 7901184 | tf_op jit(solution)/shard_map/reduce_sum | solution.py:44
  169.2 1.1 copy-done.2
  170.4 0.9 fusion.69
  171.2 0.7 pad.9
  171.9 1.1 copy.16
  173.1 0.0 copy-start.10
  173.1 42.9 %fusion.123 = bf16[1282,3072]{1,0:T(8,128)(2,1)S(1)} fusion(bf16[641,3072]{1,0:T(8,128)(2,1)S(1)} %bitcast.142, bf16[641,1282]{1,0:T(8,128)(2,1)S(1)} %copy-done), kind=kOutput, calls=%fused_computation.23.clone.clone.clone.clone.1 | convolution fusion | flops 5304895488 | bytes 13458436 | tf_op jit(solution)/shard_map/ch,cp->hp/dot_general | solution.py:48
  216.1 7.2 %fusion.18 = bf16[641,3072]{1,0:T(8,128)(2,1)S(1)} fusion(f32[641,3072]{1,0:T(8,128)S(1)} %bitcast.138, bf16[1282,641]{0,1:T(8,128)(2,1)S(1)} %copy-done.10, bf16[1282,3072]{1,0:T(8,128)(2,1)S(1)} %fusion.123), kind=kOutput, calls=%fused_computation.45 | convolution fusion | flops 5052844032 | bytes 21335044 | tf_op jit(solution)/shard_map/hc,hp->cp/dot_general | solution.py:51
  223.4 1.9 copy-done.3
  225.2 0.8 convolution_convert_fusion.1
  226.0 0.8 copy.18
  226.9 0.0 all-gather.2.cloned.1.call-update
  226.9 0.0 all-reduce.4.cloned.1.call-start
  226.9 0.1 convert_bitcast_fusion.1
  227.0 0.2 copy.17
  227.2 0.2 multiply_reduce_fusion.2
  227.4 20.9 %all-gather.2.cloned.1.call-done = bf16[4,72,24,128]{3,2,1,0:T(8,128)(2,1)} async-done(((bf16[1,72,24,128]{3,2,1,0:T(8,128)(2,1)}), bf16[4,72,24,128]{3,2,1,0:T(8,128)(2,1)}) %all-gather.2.cloned.1.call-update) | async-done | bytes 1769488 | tf_op jit(solution)/shard_map/all_gather | solution.py:64
  248.3 2.1 multiply_reduce_fusion.1
  250.4 2.0 divide_reduce_fusion
  252.5 0.2 multiply_convert_fusion.1
  252.7 2.0 convolution_multiply_fusion
  254.7 0.0 all-reduce.4.cloned.1.call-update
  254.7 0.0 all-reduce.6.cloned.1.call-start
  254.8 1.2 convolution_convert_fusion
  256.0 0.0 copy-start.1
  256.0 3.0 copy.20
  259.1 66.1 %all-reduce.4.cloned.1.call-done = f32[641,72]{0,1:T(8,128)} async-done(((f32[641,72]{0,1:T(8,128)}), f32[641,72]{0,1:T(8,128)}) %all-reduce.4.cloned.1.call-update) | async-done | bytes 184624 | tf_op jit(solution)/shard_map/psum | solution.py:80
  325.2 0.0 all-reduce.6.cloned.1.call-update
  325.2 4.7 %slice_bitcast_fusion = bf16[1,641,24,128]{3,2,1,0:T(8,128)(2,1)} fusion(bf16[648,24,128]{2,1,0:T(8,128)(2,1)} %bitcast.135), kind=kLoop, calls=%fused_computation.103 | loop fusion | bytes 7876608 | tf_op jit(solution)/shard_map/reshape | solution.py:81
  329.9 29.4 %all-reduce.6.cloned.1.call-done = f32[641,72]{0,1:T(8,128)} async-done(((f32[641,72]{0,1:T(8,128)}), f32[641,72]{0,1:T(8,128)}) %all-reduce.6.cloned.1.call-update) | async-done | bytes 184624 | tf_op jit(solution)/shard_map/psum | solution.py:80
  359.3 1.6 copy.31
  (27 shorter events, 0.2 us)
Async XLA Ops:
  7.2 165.9 %copy-start = (bf16[641,1282]{1,0:T(8,128)(2,1)S(1)}, bf16[641,1282]{1,0:T(8,128)(2,1)}, u32[]{:S(2)}) copy-start(bf16[641,1282]{1,0:T(8,128)(2,1)} %param.9) | copy-start | bytes 4930576
  7.2 241.1 %all-gather.2.cloned.1.call-start = ((), (), s32[]{:S(2)}) async-start(), calls=%async_computation | async-start | bytes 2211840 | tf_op jit(solution)/shard_map/all_gather | solution.py:64
  9.6 15.7 %collective-permute-start = (bf16[1,641,2,128]{3,1,2,0:T(8,128)(2,1)S(1)}, bf16[1,641,2,128]{3,1,2,0:T(8,128)(2,1)S(1)}, u32[]{:S(2)}, u32[]{:S(2)}) collective-permute-start(bf16[1,641,2,128]{3,1,2,0:T(8,128)(2,1)S(1)} %copy.13), channel_id=1, source_target_pairs={{0,1},{1,2},{2,3},{3,4},{4,5},{5,6},{6,7},{7,0},{8,9},{9,10},{10,1... | collective-permute-start | bytes 984584 | tf_op jit(solution)/shard_map/ppermute | solution.py:17
  11.3 16.0 %collective-permute-start.1 = (bf16[1,641,2,128]{3,1,2,0:T(8,128)(2,1)S(1)}, bf16[1,641,2,128]{3,1,2,0:T(8,128)(2,1)S(1)}, u32[]{:S(2)}, u32[]{:S(2)}) collective-permute-start(bf16[1,641,2,128]{3,1,2,0:T(8,128)(2,1)S(1)} %copy.14), channel_id=1, source_target_pairs={{1,0},{2,1},{3,2},{4,3},{5,4},{6,5},{7,6},{0,7},{9,8},{10,9},{11,1... | collective-permute-start | bytes 984584 | tf_op jit(solution)/shard_map/ppermute | solution.py:19
  15.9 5.0 %copy-start.8 = (f32[641,5,5]{0,2,1:T(8,128)S(1)}, f32[641,5,5]{0,2,1:T(8,128)}, u32[]{:S(2)}) copy-start(f32[641,5,5]{0,2,1:T(8,128)} %param.8) | copy-start | bytes 192304
  15.9 11.6 %copy-start.5 = (bf16[1,641,24,128]{3,2,1,0:T(8,128)(2,1)S(1)}, bf16[1,641,24,128]{3,2,1,0:T(8,128)(2,1)}, u32[]{:S(2)}) copy-start(bf16[1,641,24,128]{3,2,1,0:T(8,128)(2,1)} %param.7) | copy-start | bytes 11814916
  164.9 5.5 %copy-start.2 = (f32[1,641,24,128]{3,2,1,0:T(8,128)S(1)}, f32[1,641,24,128]{3,2,1,0:T(8,128)}, u32[]{:S(2)}) copy-start(f32[1,641,24,128]{3,2,1,0:T(8,128)} %get-tuple-element.28) | copy-start | bytes 23629828
  171.9 44.1 %slice-start = ((s8[7962624]{0:T(1024)(128)(4,1)}), s8[4194304]{0:T(1024)(128)(4,1)S(1)}, s32[]{:S(2)}) async-start(s8[7962624]{0:T(1024)(128)(4,1)} %bitcast.136), calls=%async_computation.3 | async-start | bytes 8388608
  173.1 43.0 %slice-start.1 = ((s8[7962624]{0:T(1024)(128)(4,1)}), s8[3768320]{0:T(1024)(128)(4,1)S(1)}, s32[]{:S(2)}) async-start(s8[7962624]{0:T(1024)(128)(4,1)} %bitcast.136), calls=%async_computation.4 | async-start | bytes 7536640
  173.1 43.0 %copy-start.10 = (bf16[1282,641]{0,1:T(8,128)(2,1)S(1)}, bf16[1282,641]{0,1:T(8,128)(2,1)}, u32[]{:S(2)}) copy-start(bf16[1282,641]{0,1:T(8,128)(2,1)} %param.10) | copy-start | bytes 4930576
  216.1 9.1 %copy-start.7 = (bf16[641,72]{0,1:T(8,128)(2,1)S(1)}, bf16[641,72]{0,1:T(8,128)(2,1)}, u32[]{:S(2)}) copy-start(bf16[641,72]{0,1:T(8,128)(2,1)} %param.11) | copy-start | bytes 276916
  223.4 1.9 copy-start.3
  225.2 1.9 copy-start.6
  225.2 2.1 copy-start.9
  226.9 98.3 %all-reduce.4.cloned.1.call-start = ((), (), s32[]{:S(2)}) async-start(), calls=%async_computation.1 | async-start | bytes 442368 | tf_op jit(solution)/shard_map/psum | solution.py:80
  248.3 4.4 %copy-start.4 = (bf16[641,3072]{1,0:T(8,128)(2,1)S(1)}, bf16[641,3072]{1,0:T(8,128)(2,1)}, u32[]{:S(2)}) copy-start(bf16[641,3072]{1,0:T(8,128)(2,1)} %copy-done.3) | copy-start | bytes 11814916
  254.7 104.6 %all-reduce.6.cloned.1.call-start = ((), (), s32[]{:S(2)}) async-start(), calls=%async_computation.2 | async-start | bytes 442368 | tf_op jit(solution)/shard_map/psum | solution.py:80
  256.0 105.0 %copy-start.1 = (bf16[641,1282]{1,0:T(8,128)(2,1)S(1)}, bf16[641,1282]{1,0:T(8,128)(2,1)}, u32[]{:S(2)}) copy-start(bf16[641,1282]{1,0:T(8,128)(2,1)} %param.9) | copy-start | bytes 4930576
Sparse Core Ops, SparseCore 0:
  227.0 21.2 all-gather.1
  254.9 70.2 all-reduce.3
  327.5 31.7 all-reduce.5
